TPU v7x, 32 devices: a whole 2x2x4 slice. The times are simulated.
32 devices in a mesh: row: 4 (over y, x), col: 8 (over z, core).
Axes of the slice: x: 2, y: 2, z: 4, core: 2. Of those that a mesh axis runs over, the one named last changes fastest.
Arguments:
- layer_input: float32 [2048, 1088], P('col', 'row'), may hold values from -6 to 6
- output_grad: float32 [2048, 1088], P('col', 'row'), may hold values from -6 to 6
- w_qkv: float32 [1088, 6144], P('row', 'col'), as said below
- w_out: float32 [2048, 1088], P('col', 'row'), as said below
- w_up: float32 [1088, 4352], P('row', 'col'), may hold values from -0.1875 to 0.1875
- w_down: float32 [4352, 1088], P('col', 'row'), may hold values from -0.09375 to 0.09375
- layernorm_params: float32 [4, 1088], P(None, 'row')
- state_qkv: float32 [2, 1088, 6144], P(None, 'row', 'col'), as said below
- state_out: float32 [2, 2048, 1088], P(None, 'col', 'row'), as said below
- state_up: float32 [2, 1088, 4352], P(None, 'row', 'col'), as said below
- state_down: float32 [2, 4352, 1088], P(None, 'col', 'row'), as said below
- state_norms: float32 [2, 4, 1088], P(None, None, 'row'), as said below
- segment_ids: int32 [4, 512], P('row'), may hold values from 0 to 2, as said below
Outputs:
- block_output: float32 [2048, 1088], P('col', 'row')
- layer_input_grad: float32 [2048, 1088], P('col', 'row')
- grad_qkv: float32 [1088, 6144], P('row', 'col')
- grad_out: float32 [2048, 1088], P('col', 'row')
- grad_up: float32 [1088, 4352], P('row', 'col')
- grad_down: float32 [4352, 1088], P('col', 'row')
- norm_params_grad: float32 [4, 1088], P(None, 'row')
- new_qkv: float32 [1088, 6144], P('row', 'col')
- new_out: float32 [2048, 1088], P('col', 'row')
- new_up: float32 [1088, 4352], P('row', 'col')
- new_down: float32 [4352, 1088], P('col', 'row')
- new_norms: float32 [4, 1088], P(None, 'row')
- next_state_qkv: float32 [2, 1088, 6144], P(None, 'row', 'col')
- next_state_out: float32 [2, 2048, 1088], P(None, 'col', 'row')
- next_state_up: float32 [2, 1088, 4352], P(None, 'row', 'col')
- next_state_down: float32 [2, 4352, 1088], P(None, 'col', 'row')
- next_state_norms: float32 [2, 4, 1088], P(None, None, 'row')
Inputs may be any that keep to these rules, and one draw needn't show every extreme that they name: `segment_ids`: within each sequence the ids never fall; each sequence holds exactly three documents, numbered 0, 1, 2, the first two of 64 or more tokens. `w_qkv`: columns of heads 17 and above are zero. `w_out`: rows of heads 17 and above are zero. `state_qkv`: both moments are zero in the columns of heads 17 and above; second moments are positive elsewhere. `state_out`: both moments are zero in the rows of heads 17 and above; second moments are positive elsewhere. `state_up`: second moments are positive. `state_down`: second moments are positive. `state_norms`: second moments are positive.
All inputs are finite; a program needn't handle non-finite values.
Results may differ from a plain program's by a relative error of at most 0.011.
Values may be sent and summed in bfloat16 or wider, within the bound.
No kernel may reach another device: no remote copies, remote signals or barrier semaphores. Data moves between devices by JAX's collectives and lax.ppermute only.
A program may use at most 128 MiB of HBM per device.

v0:
```python
import jax
import jax.numpy as jnp
from jax import lax
from jax.sharding import PartitionSpec as P

MODEL_WIDTH = 1088
HS = 64
SEQ = 512
EPS_NORM = 1e-05
NEG_FILL = -1e30
BETA_ONE = 0.9
BETA_TWO = 0.95
RATE = 0.01
DECAY = 0.1
STEP_COUNT = 3
ADAM_EPS = 1e-08


def row_product(left, right):
    return lax.dot_general(
        left, right, (((0,), (0,)), ((), ())), preferred_element_type=jnp.float32
    )


def back_product(left, right):
    return lax.dot_general(
        left, right, (((1,), (1,)), ((), ())), preferred_element_type=jnp.float32
    )


def layernorm_forward(x, norm_gain, shift_bias):
    total = lax.psum(jnp.sum(x, axis=1), "row")
    mean_removed = x - (total / MODEL_WIDTH)[:, None]
    spread = lax.psum(jnp.sum(mean_removed * mean_removed, axis=1), "row")
    inverse_deviation = lax.rsqrt(spread / MODEL_WIDTH + EPS_NORM)[:, None]
    normalized_rows = mean_removed * inverse_deviation
    return (
        normalized_rows,
        inverse_deviation,
        (normalized_rows * norm_gain + shift_bias).astype(jnp.bfloat16),
    )


def layernorm_backward(incoming_grad, normalized_rows, inverse_deviation, norm_gain):
    normalized_grad = incoming_grad * norm_gain
    first_branch, second_branch = lax.psum(
        (jnp.sum(normalized_grad, axis=1), jnp.sum(normalized_grad * normalized_rows, axis=1)),
        "row",
    )
    return inverse_deviation * (
        normalized_grad
        - (first_branch / MODEL_WIDTH)[:, None]
        - normalized_rows * (second_branch / MODEL_WIDTH)[:, None]
    )


def activation(value):
    return jax.nn.gelu(value, approximate=True)


def slope(value, incoming_grad):
    return jax.vjp(activation, value)[1](incoming_grad)[0]


def spread_in(acts, weight):
    gathered = lax.all_gather(acts, "col", axis=0, tiled=True)
    widened = lax.all_to_all(gathered, "row", split_axis=0, concat_axis=1, tiled=True)
    whole = lax.all_gather(weight, "row", axis=0, tiled=True)
    return ((widened, whole), jnp.dot(widened, whole, preferred_element_type=jnp.float32))


def spread_out(branch, weight):
    gathered = lax.all_gather(branch, "row", axis=0, tiled=True)
    return (
        gathered,
        lax.psum_scatter(
            jnp.dot(gathered, weight, preferred_element_type=jnp.float32),
            "col",
            scatter_dimension=0,
            tiled=True,
        ),
    )


def back_in(grad, kept):
    widened, whole = kept
    weight_grad = lax.psum_scatter(
        row_product(widened, grad), "row", scatter_dimension=0, tiled=True
    )
    partial_value = back_product(grad, whole)
    moved = lax.all_to_all(partial_value, "row", split_axis=1, concat_axis=0, tiled=True)
    return (weight_grad, lax.psum_scatter(moved, "col", scatter_dimension=0, tiled=True))


def back_out(grad, gathered, weight):
    full = lax.all_gather(grad, "col", axis=0, tiled=True)
    weight_grad = row_product(gathered, full)
    return (
        weight_grad,
        lax.psum_scatter(back_product(full, weight), "row", scatter_dimension=0, tiled=True),
    )


def masked_scores(query, keys, segment):
    scores = jnp.einsum("qhd,khd->hqk", query, keys, preferred_element_type=jnp.float32) * HS ** (
        -0.5
    )
    place = jnp.arange(segment.shape[0])
    allowed = (place[None, :] <= place[:, None]) & (segment[None, :] == segment[:, None])
    return jnp.where(allowed[None], scores, NEG_FILL)


def attend(item):
    block, segment = item
    query, keys, values = (block[:, :, 0], block[:, :, 1], block[:, :, 2])
    scores = masked_scores(query, keys, segment)
    top = jnp.max(scores, axis=-1)
    lse = top + jnp.log(jnp.sum(jnp.exp(scores - top[..., None]), axis=-1))
    probs = jnp.exp(scores - lse[..., None]).astype(jnp.bfloat16)
    result = jnp.einsum("hqk,khd->qhd", probs, values, preferred_element_type=jnp.float32)
    return (result.astype(jnp.bfloat16), lse)


def attend_back(item):
    block, segment, lse, incoming_grad = item
    query, keys, values = (block[:, :, 0], block[:, :, 1], block[:, :, 2])
    probs = jnp.exp(masked_scores(query, keys, segment) - lse[..., None])
    probs_low = probs.astype(jnp.bfloat16)
    dvalues = jnp.einsum(
        "hqk,qhd->khd", probs_low, incoming_grad, preferred_element_type=jnp.float32
    )
    dprobs = jnp.einsum("qhd,khd->hqk", incoming_grad, values, preferred_element_type=jnp.float32)
    delta = jnp.sum(probs * dprobs, axis=-1, keepdims=True)
    dscores = (probs * (dprobs - delta)).astype(jnp.bfloat16)
    dquery = jnp.einsum("hqk,khd->qhd", dscores, keys, preferred_element_type=jnp.float32) * HS ** (
        -0.5
    )
    dkeys = jnp.einsum("hqk,qhd->khd", dscores, query, preferred_element_type=jnp.float32) * HS ** (
        -0.5
    )
    return jnp.stack([dquery, dkeys, dvalues], axis=2).astype(jnp.bfloat16)


def adamw(param, grad, state, decay):
    first_branch = BETA_ONE * state[0] + (1.0 - BETA_ONE) * grad
    second_branch = BETA_TWO * state[1] + (1.0 - BETA_TWO) * grad * grad
    first_hat = first_branch / (1.0 - BETA_ONE**STEP_COUNT)
    second_hat = second_branch / (1.0 - BETA_TWO**STEP_COUNT)
    updated = param - RATE * (first_hat / (jnp.sqrt(second_hat) + ADAM_EPS) + decay * param)
    return (updated, jnp.stack([first_branch, second_branch]))


def shards(
    layer_input,
    output_grad,
    w_qkv,
    w_out,
    w_up,
    w_down,
    layernorm_params,
    state_qkv,
    state_out,
    state_up,
    state_down,
    state_norms,
    segment_ids,
):
    low = jnp.bfloat16
    wq, wo, wu, wd = (w_qkv.astype(low), w_out.astype(low), w_up.astype(low), w_down.astype(low))
    local_seqs = segment_ids.shape[0]
    normalized_rows1, inverse_deviation1, attention_input = layernorm_forward(
        layer_input, layernorm_params[0], layernorm_params[1]
    )
    kept_first, qkv_sum = spread_in(attention_input, wq)
    blocks = qkv_sum.astype(low).reshape(local_seqs, SEQ, -1, 3, HS)
    attended, lse = lax.map(attend, (blocks, segment_ids))
    attended = attended.reshape(local_seqs * SEQ, -1)
    kept_attended, attn_sum = spread_out(attended, wo)
    middle_stream = layer_input + attn_sum
    normalized_rows2, inverse_deviation2, feedforward_input = layernorm_forward(
        middle_stream, layernorm_params[2], layernorm_params[3]
    )
    kept_second, pre = spread_in(feedforward_input, wu)
    hidden = activation(pre).astype(low)
    kept_hidden, mlp_sum = spread_out(hidden, wd)
    block_output = middle_stream + mlp_sum
    out_low = output_grad.astype(low)
    grad_down, hidden_grad = back_out(out_low, kept_hidden, wd)
    pre_grad = slope(pre, hidden_grad).astype(low)
    grad_up, feedforward_input_grad = back_in(pre_grad, kept_second)
    middle_stream_grad = output_grad + layernorm_backward(
        feedforward_input_grad, normalized_rows2, inverse_deviation2, layernorm_params[2]
    )
    middle_low = middle_stream_grad.astype(low)
    grad_out, attended_grad = back_out(middle_low, kept_attended, wo)
    incoming_grad = attended_grad.astype(low).reshape(local_seqs, SEQ, -1, HS)
    qkv_grad = lax.map(attend_back, (blocks, segment_ids, lse, incoming_grad)).reshape(
        local_seqs * SEQ, -1
    )
    grad_qkv, attention_input_grad = back_in(qkv_grad, kept_first)
    layer_input_grad = middle_stream_grad + layernorm_backward(
        attention_input_grad, normalized_rows1, inverse_deviation1, layernorm_params[0]
    )
    local_terms = jnp.stack(
        [
            jnp.sum(attention_input_grad * normalized_rows1, axis=0),
            jnp.sum(attention_input_grad, axis=0),
            jnp.sum(feedforward_input_grad * normalized_rows2, axis=0),
            jnp.sum(feedforward_input_grad, axis=0),
        ]
    )
    norm_params_grad = lax.psum(local_terms, "col")
    new_qkv, next_state_qkv = adamw(w_qkv, grad_qkv, state_qkv, DECAY)
    new_out, next_state_out = adamw(w_out, grad_out, state_out, DECAY)
    new_up, next_state_up = adamw(w_up, grad_up, state_up, DECAY)
    new_down, next_state_down = adamw(w_down, grad_down, state_down, DECAY)
    new_norms, next_state_norms = adamw(layernorm_params, norm_params_grad, state_norms, 0.0)
    return (
        block_output,
        layer_input_grad,
        grad_qkv,
        grad_out,
        grad_up,
        grad_down,
        norm_params_grad,
        new_qkv,
        new_out,
        new_up,
        new_down,
        new_norms,
        next_state_qkv,
        next_state_out,
        next_state_up,
        next_state_down,
        next_state_norms,
    )


def solution(mesh):
    placed = (
        P("col", "row"),
        P("col", "row"),
        P("row", "col"),
        P("col", "row"),
        P("row", "col"),
        P("col", "row"),
        P(None, "row"),
        P(None, "row", "col"),
        P(None, "col", "row"),
        P(None, "row", "col"),
        P(None, "col", "row"),
        P(None, None, "row"),
        P("row", None),
    )
    return jax.shard_map(
        shards,
        mesh=mesh,
        in_specs=placed,
        out_specs=(
            P("col", "row"),
            P("col", "row"),
            P("row", "col"),
            P("col", "row"),
            P("row", "col"),
            P("col", "row"),
            P(None, "row"),
            P("row", "col"),
            P("col", "row"),
            P("row", "col"),
            P("col", "row"),
            P(None, "row"),
            P(None, "row", "col"),
            P(None, "col", "row"),
            P(None, "row", "col"),
            P(None, "col", "row"),
            P(None, None, "row"),
        ),
        check_vma=False,
    )
```

profile of v0, /device:TPU:0, one launch (start us, length us, event | category | flops | bytes accessed | tf_op | source)
XLA Modules:
  0.0 672.1 jit_solution(4915500629032504406)
XLA Ops:
  7.2 1.1 reduce_sum.128
  8.3 11.4 %psum.63 = f32[256]{0:T(256)S(1)} all-reduce(f32[256]{0:T(256)S(1)} %reduce_sum.128), channel_id=1, replica_groups=mesh['row'=4,'col'=8] {'row'}, use_global_device_ids=true, to_apply=%region_1.0 | all-reduce | flops 256 | bytes 2048 | tf_op jit(solution)/shard_map/psum | solution.py:32
  19.7 1.0 multiply_reduce_fusion.6
  20.7 8.0 %psum.64 = f32[256]{0:T(256)S(1)} all-reduce(f32[256]{0:T(256)S(1)} %multiply_reduce_fusion.6), channel_id=1, replica_groups=mesh['row'=4,'col'=8] {'row'}, use_global_device_ids=true, to_apply=%region_3.0 | all-reduce | flops 256 | bytes 2048 | tf_op jit(solution)/shard_map/psum | solution.py:34
  29.6 1.8 add_convert_fusion.1
  32.2 23.8 %all-gather.9.cloned.1.call-done = bf16[2048,272]{0,1:T(8,128)(2,1)} async-done(((bf16[256,272]{0,1:T(8,128)(2,1)}), bf16[2048,272]{0,1:T(8,128)(2,1)}) %all-gather.9.cloned.1.call-update) | async-done | bytes 1114128 | tf_op jit(solution)/shard_map/all_gather | solution.py:66
  56.1 2.3 copy.87
  58.4 3.7 all-to-all-start
  62.3 35.0 %all-gather.11.cloned.1.call-done = bf16[1088,768]{1,0:T(8,128)(2,1)} async-done(((bf16[272,768]{1,0:T(8,128)(2,1)}), bf16[1088,768]{1,0:T(8,128)(2,1)}) %all-gather.11.cloned.1.call-update) | async-done | bytes 1671184 | tf_op jit(solution)/shard_map/all_gather | solution.py:68
  97.3 3.6 convolution_convert_fusion
  100.9 1.4 copy.57
  105.2 2.0 convolution_convert_fusion.2
  107.2 26.5 %all-gather.13.cloned.1.call-done = bf16[2048,256]{0,1:T(8,128)(2,1)} async-done(((bf16[512,256]{0,1:T(8,128)(2,1)}), bf16[2048,256]{0,1:T(8,128)(2,1)}) %all-gather.13.cloned.1.call-update) | async-done | bytes 1048592 | tf_op jit(solution)/shard_map/all_gather | solution.py:73
  133.7 3.1 fusion.34
  138.5 34.9 %reduce-scatter.11.cloned.1.call-done = f32[256,272]{0,1:T(8,128)} async-done(((f32[2048,272]{0,1:T(8,128)}), f32[256,272]{0,1:T(8,128)}) %reduce-scatter.11.cloned.1.call-update) | async-done | bytes 278544 | tf_op jit(solution)/shard_map/reduce_scatter | solution.py:76
  173.4 1.0 fusion.43
  174.4 9.8 %psum.65 = f32[256]{0:T(256)S(1)} all-reduce(f32[256]{0:T(256)S(1)} %get-tuple-element.68), channel_id=1, replica_groups=mesh['row'=4,'col'=8] {'row'}, use_global_device_ids=true, to_apply=%region_8.9 | all-reduce | flops 256 | bytes 2048 | tf_op jit(solution)/shard_map/psum | solution.py:32
  184.4 8.2 %psum.66 = f32[256]{0:T(256)S(1)} all-reduce(f32[256]{0:T(256)S(1)} %multiply_reduce_fusion.5), channel_id=1, replica_groups=mesh['row'=4,'col'=8] {'row'}, use_global_device_ids=true, to_apply=%region_10.11 | all-reduce | flops 256 | bytes 2048 | tf_op jit(solution)/shard_map/psum | solution.py:34
  194.3 4.3 all-gather.21.cloned.1.call-done
  198.6 4.7 fusion.24
  203.4 20.2 %all-gather.15.cloned.1.call-done = bf16[2048,272]{0,1:T(8,128)(2,1)} async-done(((bf16[256,272]{0,1:T(8,128)(2,1)}), bf16[2048,272]{0,1:T(8,128)(2,1)}) %all-gather.15.cloned.1.call-update) | async-done | bytes 1114128 | tf_op jit(solution)/shard_map/all_gather | solution.py:66
  223.6 2.3 copy.86
  225.9 3.5 all-to-all-start.1
  229.5 33.0 %all-gather.17.cloned.1.call-done = bf16[1088,544]{1,0:T(8,128)(2,1)} async-done(((bf16[272,544]{1,0:T(8,128)(2,1)}), bf16[1088,544]{1,0:T(8,128)(2,1)}) %all-gather.17.cloned.1.call-update) | async-done | bytes 1183760 | tf_op jit(solution)/shard_map/all_gather | solution.py:68
  262.5 57.9 %reduce-scatter.15.cloned.1.call-done = f32[512,544]{0,1:T(8,128)} async-done(((f32[2048,544]{0,1:T(8,128)}), f32[512,544]{0,1:T(8,128)}) %reduce-scatter.15.cloned.1.call-update) | async-done | bytes 1114128 | tf_op jit(solution)/shard_map/reduce_scatter | solution.py:100
  320.4 4.3 fusion.13
  324.7 2.5 fusion.49
  327.2 36.8 %all_to_all.73 = f32[512,4,272]{0,2,1:T(8,128)S(1)} all-to-all(f32[512,4,272]{0,2,1:T(8,128)S(1)} %bitcast.188), channel_id=1, replica_groups=mesh['row'=4,'col'=8] {'row'}, dimensions={1} | all-to-all | bytes 4456448 | tf_op jit(solution)/shard_map/all_to_all | solution.py:91
  364.0 1.6 copy.82
  365.7 8.5 %all-gather.19.cloned.1.call-done = bf16[2048,544]{0,1:T(8,128)(2,1)} async-done(((bf16[512,544]{0,1:T(8,128)(2,1)}), bf16[2048,544]{0,1:T(8,128)(2,1)}) %all-gather.19.cloned.1.call-update) | async-done | bytes 2228240 | tf_op jit(solution)/shard_map/all_gather | solution.py:73
  374.2 4.0 fusion.26
  378.3 34.5 %reduce-scatter.17.cloned.1.call-done = f32[256,272]{0,1:T(8,128)} async-done(((f32[2048,272]{0,1:T(8,128)}), f32[256,272]{0,1:T(8,128)}) %reduce-scatter.17.cloned.1.call-update) | async-done | bytes 278544 | tf_op jit(solution)/shard_map/reduce_scatter | solution.py:92
  412.8 1.2 multiply_reduce_fusion.1
  414.0 10.2 %all-reduce.2 = (f32[256]{0:T(256)S(1)}, f32[256]{0:T(256)S(1)}) all-reduce(f32[256]{0:T(256)S(1)} %get-tuple-element.53, f32[256]{0:T(256)S(1)} %get-tuple-element.54), channel_id=1, replica_groups=mesh['row'=4,'col'=8] {'row'}, use_global_device_ids=true, to_apply=%region_17.18 | all-reduce | flops 512 | bytes 4096 | tf_op jit(solution)/shard_map/psum | solution.py:46
  424.2 26.2 %reduce-scatter.13.cloned.1.call-done = f32[256,272]{0,1:T(8,128)} async-done(((f32[2048,272]{0,1:T(8,128)}), f32[256,272]{0,1:T(8,128)}) %reduce-scatter.13.cloned.1.call-update) | async-done | bytes 278544 | tf_op jit(solution)/shard_map/reduce_scatter | solution.py:76
  450.4 2.1 fusion.42
  452.6 23.1 %all-gather.23.cloned.1.call-done = bf16[2048,272]{0,1:T(8,128)(2,1)} async-done(((bf16[256,272]{0,1:T(8,128)(2,1)}), bf16[2048,272]{0,1:T(8,128)(2,1)}) %all-gather.23.cloned.1.call-update) | async-done | bytes 1114128 | tf_op jit(solution)/shard_map/all_gather | solution.py:96
  475.7 3.4 fusion.32
  479.2 3.8 fusion.47
  483.0 30.2 %reduce-scatter.19.cloned.1.call-done = f32[512,256]{1,0:T(8,128)} async-done(((f32[2048,256]{1,0:T(8,128)}), f32[512,256]{1,0:T(8,128)}) %reduce-scatter.19.cloned.1.call-update) | async-done | bytes 524304 | tf_op jit(solution)/shard_map/reduce_scatter | solution.py:100
  513.2 1.8 convert_element_type.83
  515.0 1.1 copy.64
  516.1 3.9 multiply_reduce_fusion
  520.0 1.3 multiply_convert_fusion
  522.5 1.3 fusion.6
  523.9 1.3 copy-done.28
  525.2 1.0 fusion.44
  526.2 38.4 %all_to_all.74 = f32[512,4,272]{0,2,1:T(8,128)S(1)} all-to-all(f32[512,4,272]{0,2,1:T(8,128)S(1)} %fusion.44), channel_id=1, replica_groups=mesh['row'=4,'col'=8] {'row'}, dimensions={1} | all-to-all | bytes 4456448 | tf_op jit(solution)/shard_map/all_to_all | solution.py:91
  564.6 1.6 copy.83
  566.2 2.8 fusion.45
  569.0 1.2 copy-done.14
  570.3 2.9 fusion.48
  573.2 1.4 fusion.23
  574.6 1.2 pad_maximum_fusion.2
  576.6 2.5 fusion.22
  579.1 1.2 pad_maximum_fusion.1
  583.5 29.9 %reduce-scatter.21.cloned.1.call-done = f32[256,272]{0,1:T(8,128)} async-done(((f32[2048,272]{0,1:T(8,128)}), f32[256,272]{0,1:T(8,128)}) %reduce-scatter.21.cloned.1.call-update) | async-done | bytes 278544 | tf_op jit(solution)/shard_map/reduce_scatter | solution.py:92
  613.4 1.2 multiply_reduce_fusion.2
  614.6 9.8 %all-reduce.1 = (f32[256]{0:T(256)S(1)}, f32[256]{0:T(256)S(1)}) all-reduce(f32[256]{0:T(256)S(1)} %get-tuple-element.51, f32[256]{0:T(256)S(1)} %get-tuple-element.55), channel_id=1, replica_groups=mesh['row'=4,'col'=8] {'row'}, use_global_device_ids=true, to_apply=%region_24.25 | all-reduce | flops 512 | bytes 4096 | tf_op jit(solution)/shard_map/psum | solution.py:46
  624.5 13.9 %psum.71 = f32[4,272]{1,0:T(4,128)S(1)} all-reduce(f32[4,272]{1,0:T(4,128)S(1)} %pad_maximum_fusion.6), channel_id=1, replica_groups=mesh['row'=4,'col'=8] {'col'}, use_global_device_ids=true, to_apply=%region_31.32 | all-reduce | flops 1088 | bytes 8704 | tf_op jit(solution)/shard_map/psum | solution.py:212
  639.6 1.8 multiply_add_fusion
  641.4 19.7 %reduce-scatter.23.cloned.1.call-done = f32[272,768]{1,0:T(8,128)} async-done(((f32[1088,768]{1,0:T(8,128)}), f32[272,768]{1,0:T(8,128)}) %reduce-scatter.23.cloned.1.call-update) | async-done | bytes 835600 | tf_op jit(solution)/shard_map/reduce_scatter | solution.py:87
  661.1 3.2 fusion.21
  664.3 1.3 pad_maximum_fusion
  (122 shorter events, 15.6 us)
Async XLA Ops:
  7.2 24.2 %copy-start.10 = (f32[272,768]{1,0:T(8,128)S(1)}, f32[272,768]{1,0:T(8,128)}, u32[]{:S(2)}) copy-start(f32[272,768]{1,0:T(8,128)} %param.15) | copy-start | bytes 2506756
  7.2 48.9 %all-gather.9.cloned.1.call-start = ((), (), s32[]{:S(2)}) async-start(), calls=%async_computation.12 | async-start | bytes 1253376 | tf_op jit(solution)/shard_map/all_gather | solution.py:66
  31.4 66.0 %all-gather.11.cloned.1.call-start = ((), (), s32[]{:S(2)}) async-start(), calls=%async_computation.13 | async-start | bytes 2088960 | tf_op jit(solution)/shard_map/all_gather | solution.py:68
  58.4 3.7 copy-start.27
  58.4 38.9 %all-to-all-start = ((bf16[4,512,272]{1,2,0:T(8,128)(2,1)}), bf16[4,512,272]{1,2,0:T(8,128)(2,1)S(1)}, u32[]{:S(2)}, u32[]{:S(2)}) async-start(bf16[4,512,272]{1,2,0:T(8,128)(2,1)} %bitcast.171), calls=%async_computation | async-start | bytes 2228224 | tf_op jit(solution)/shard_map/all_to_all | solution.py:67
  62.1 71.7 %all-gather.13.cloned.1.call-start = ((), (), s32[]{:S(2)}) async-start(), calls=%async_computation.14 | async-start | bytes 1310720 | tf_op jit(solution)/shard_map/all_gather | solution.py:73
  62.3 41.9 %copy-start.8 = (pred[512,512]{0,1:T(8,128)(4,1)}, pred[512,512]{0,1:T(8,128)(4,1)S(1)}, u32[]{:S(2)}) copy-start(pred[512,512]{0,1:T(8,128)(4,1)S(1)} %fusion.14) | copy-start | bytes 786436
  102.3 1.9 copy-start.12
  103.2 2.0 copy-start
  105.2 28.5 %copy-start.5 = (f32[256,272]{0,1:T(8,128)S(1)}, f32[256,272]{0,1:T(8,128)}, u32[]{:S(2)}) copy-start(f32[256,272]{0,1:T(8,128)} %param.16) | copy-start | bytes 835588
  107.2 66.2 %reduce-scatter.11.cloned.1.call-start = ((), (), s32[]{:S(2)}) async-start(), calls=%async_computation.15 | async-start | bytes 2506752 | tf_op jit(solution)/shard_map/reduce_scatter | solution.py:76
  136.8 1.0 copy-start.19
  136.8 36.6 %copy-start.2 = (f32[256,272]{0,1:T(8,128)S(1)}, f32[256,272]{0,1:T(8,128)}, u32[]{:S(2)}) copy-start(f32[256,272]{0,1:T(8,128)} %param.13) | copy-start | bytes 835588
  136.9 56.6 %copy-start.15 = (f32[272,544]{1,0:T(8,128)S(1)}, f32[272,544]{1,0:T(8,128)}, u32[]{:S(2)}) copy-start(f32[272,544]{1,0:T(8,128)} %param.17) | copy-start | bytes 1775620
  136.9 61.7 %all-gather.21.cloned.1.call-start = ((), (), s32[]{:S(2)}) async-start(), calls=%async_computation.20 | async-start | bytes 1253376 | tf_op jit(solution)/shard_map/all_gather | solution.py:96
  138.5 60.1 %copy-start.3 = (f32[544,272]{0,1:T(8,128)S(1)}, f32[544,272]{0,1:T(8,128)}, u32[]{:S(2)}) copy-start(f32[544,272]{0,1:T(8,128)} %param.18) | copy-start | bytes 1775620
  138.5 85.1 %all-gather.15.cloned.1.call-start = ((), (), s32[]{:S(2)}) async-start(), calls=%async_computation.16 | async-start | bytes 1253376 | tf_op jit(solution)/shard_map/all_gather | solution.py:66
  193.4 69.1 %all-gather.17.cloned.1.call-start = ((), (), s32[]{:S(2)}) async-start(), calls=%async_computation.17 | async-start | bytes 1740800 | tf_op jit(solution)/shard_map/all_gather | solution.py:68
  194.2 126.1 %reduce-scatter.15.cloned.1.call-start = ((), (), s32[]{:S(2)}) async-start(), calls=%async_computation.21 | async-start | bytes 5570560 | tf_op jit(solution)/shard_map/reduce_scatter | solution.py:100
  225.9 94.4 %all-to-all-start.1 = ((bf16[4,512,272]{1,2,0:T(8,128)(2,1)}), bf16[4,512,272]{1,2,0:T(8,128)(2,1)S(1)}, u32[]{:S(2)}, u32[]{:S(2)}) async-start(bf16[4,512,272]{1,2,0:T(8,128)(2,1)} %bitcast.180), calls=%async_computation.2 | async-start | bytes 2228224 | tf_op jit(solution)/shard_map/all_to_all | solution.py:67
  229.5 144.7 %all-gather.19.cloned.1.call-start = ((), (), s32[]{:S(2)}) async-start(), calls=%async_computation.18 | async-start | bytes 2785280 | tf_op jit(solution)/shard_map/all_gather | solution.py:73
  324.7 88.1 %reduce-scatter.17.cloned.1.call-start = ((), (), s32[]{:S(2)}) async-start(), calls=%async_computation.22 | async-start | bytes 2506752 | tf_op jit(solution)/shard_map/reduce_scatter | solution.py:92
  365.7 84.7 %reduce-scatter.13.cloned.1.call-start = ((), (), s32[]{:S(2)}) async-start(), calls=%async_computation.19 | async-start | bytes 2506752 | tf_op jit(solution)/shard_map/reduce_scatter | solution.py:76
  378.2 97.5 %all-gather.23.cloned.1.call-start = ((), (), s32[]{:S(2)}) async-start(), calls=%async_computation.23 | async-start | bytes 1253376 | tf_op jit(solution)/shard_map/all_gather | solution.py:96
  452.5 60.6 %reduce-scatter.19.cloned.1.call-start = ((), (), s32[]{:S(2)}) async-start(), calls=%async_computation.24 | async-start | bytes 2621440 | tf_op jit(solution)/shard_map/reduce_scatter | solution.py:100
  479.1 96.6 %reduce-scatter.25.cloned.1.call-start = ((), (), s32[]{:S(2)}) async-start(), calls=%async_computation.27 | async-start | bytes 3481600
  482.9 33.1 %copy-start.9 = (pred[512,512]{0,1:T(8,128)(4,1)S(1)}, pred[512,512]{0,1:T(8,128)(4,1)}, u32[]{:S(2)}) copy-start(pred[512,512]{0,1:T(8,128)(4,1)} %copy-done.8) | copy-start | bytes 786436
  482.9 33.1 %copy-start.13 = (bf16[512,768]{0,1:T(8,128)(2,1)S(1)}, bf16[512,768]{0,1:T(8,128)(2,1)}, u32[]{:S(2)}) copy-start(bf16[512,768]{0,1:T(8,128)(2,1)} %copy-done.12) | copy-start | bytes 2359300
  483.0 130.4 %reduce-scatter.21.cloned.1.call-start = ((), (), s32[]{:S(2)}) async-start(), calls=%async_computation.25 | async-start | bytes 2506752 | tf_op jit(solution)/shard_map/reduce_scatter | solution.py:92
  516.1 3.9 copy-start.1
  523.7 1.4 copy-start.28
  566.2 94.9 %reduce-scatter.23.cloned.1.call-start = ((), (), s32[]{:S(2)}) async-start(), calls=%async_computation.26 | async-start | bytes 4177920 | tf_op jit(solution)/shard_map/reduce_scatter | solution.py:87
  569.0 1.3 copy-start.14
  570.3 2.9 copy-start.17
  573.1 1.4 copy-start.22
  574.5 1.3 copy-start.16
  574.6 2.1 copy-start.18
  579.1 1.8 copy-start.4
  579.1 2.1 copy-start.7
  580.3 1.4 copy-start.6
  580.3 1.4 copy-start.23
  581.7 32.9 %copy-start.21 = (f32[256,272]{0,1:T(8,128)}, f32[256,272]{0,1:T(8,128)S(1)}, u32[]{:S(2)}) copy-start(f32[256,272]{0,1:T(8,128)S(1)} %fusion.46) | copy-start | bytes 835588
  581.7 56.7 %copy-start.24 = (f32[4,272]{1,0:T(4,128)S(1)}, f32[4,272]{1,0:T(4,128)}, u32[]{:S(2)}) copy-start(f32[4,272]{1,0:T(4,128)} %param.19) | copy-start | bytes 13060
  581.7 56.7 %copy-start.26 = (f32[2,4,272]{2,1,0:T(4,128)S(1)}, f32[2,4,272]{2,1,0:T(4,128)}, u32[]{:S(2)}) copy-start(f32[2,4,272]{2,1,0:T(4,128)} %param.24) | copy-start | bytes 26116
  581.7 57.9 %copy-start.20 = (f32[256,272]{0,1:T(8,128)S(1)}, f32[256,272]{0,1:T(8,128)}, u32[]{:S(2)}) copy-start(f32[256,272]{0,1:T(8,128)} %get-tuple-element.67) | copy-start | bytes 835588
  582.7 78.4 %copy-start.11 = (f32[272,768]{1,0:T(8,128)S(1)}, f32[272,768]{1,0:T(8,128)}, u32[]{:S(2)}) copy-start(f32[272,768]{1,0:T(8,128)} %param.15) | copy-start | bytes 2506756
  638.4 25.9 %copy-start.25 = (f32[4,272]{1,0:T(4,128)}, f32[4,272]{1,0:T(4,128)S(1)}, u32[]{:S(2)}) copy-start(f32[4,272]{1,0:T(4,128)S(1)} %psum.71) | copy-start | bytes 13060
Sparse Core Ops, SparseCore 0:
  31.5 24.5 all-gather.8
  58.5 38.8 all-gather.10
  107.3 26.3 all-gather.12
  137.0 36.3 reduce-scatter.10
  175.4 23.1 all-gather.20
  200.6 22.9 all-gather.14
  226.0 36.4 all-gather.16
  265.6 54.7 reduce-scatter.14
  324.8 49.3 all-gather.18
  376.3 36.4 reduce-scatter.16
  415.1 35.2 reduce-scatter.12
  452.7 23.0 all-gather.22
  479.3 33.8 reduce-scatter.18
  516.6 57.8 reduce-scatter.24
  576.7 36.6 reduce-scatter.20
  616.9 44.1 reduce-scatter.22
where the time goes:
time: 674 us; the launch traced here: 672 us
  waiting for transfers between devices  408 us (61%)
  blocking collectives  146 us (22%)
  matrix products  45.7 us (7%)
  other arithmetic  32.3 us (5%)
  local copies, waits for them, and re-layouts  17.5 us (3%)
  between operations  14.4 us (2%)
  starting transfers between devices  7.85 us (1%)
    reduce_scatter x2, waiting for transfers between devices, back_out(): lax.psum_scatter(back_product(full, weight), 'row', scatter_dimension=0,...  88 us
    all_to_all x2, blocking collectives, back_in(): lax.all_to_all(partial_value, 'row', split_axis=1, concat_axis=0, tiled=T...  75.2 us
    all_gather x2, waiting for transfers between devices, spread_in(): whole = lax.all_gather(weight, 'row', axis=0, tiled=True)  68 us
    reduce_scatter x2, waiting for transfers between devices, back_in(): lax.psum_scatter(moved, 'col', scatter_dimension=0, tiled=True)  64.4 us
    reduce_scatter x2, waiting for transfers between devices, spread_out(): lax.psum_scatter(jnp.dot(gathered, weight, preferred_element_type=jnp.flo...  61.1 us
    all_gather x2, waiting for transfers between devices, spread_in(): gathered = lax.all_gather(acts, 'col', axis=0, tiled=True)  44.1 us
    all_gather x2, waiting for transfers between devices, spread_out(): gathered = lax.all_gather(branch, 'row', axis=0, tiled=True)  34.9 us
    all_gather x2, waiting for transfers between devices, back_out(): full = lax.all_gather(grad, 'col', axis=0, tiled=True)  27.5 us
  transfers between devices with their start and end apart: 18, of which 15 were waited for; matrix products, arithmetic and copies ran while one was open for 9% of the time, Pallas kernels for 0%

commit v1 on v0

--- a/solution.py
+++ b/solution.py
@@ -88,7 +88,12 @@
         row_product(widened, grad), "row", scatter_dimension=0, tiled=True
     )
     partial_value = back_product(grad, whole)
-    moved = lax.all_to_all(partial_value, "row", split_axis=1, concat_axis=0, tiled=True)
+    moved = jnp.concatenate(
+        lax.all_to_all(
+            jnp.stack(jnp.split(partial_value, lax.axis_size("row"), axis=1)), "row", 0, 0
+        ),
+        axis=0,
+    )
     return (weight_grad, lax.psum_scatter(moved, "col", scatter_dimension=0, tiled=True))
 
 

time: 674 us -> 671 us (level)
  no operation moved by 1% of the time
where the time goes in v1:
time: 671 us; the launch traced here: 669 us
  waiting for transfers between devices  405 us (60%)
  blocking collectives  146 us (22%)
  matrix products  44.7 us (7%)
  other arithmetic  33.3 us (5%)
  local copies, waits for them, and re-layouts  16.8 us (3%)
  between operations  14.4 us (2%)
  starting transfers between devices  8.11 us (1%)
    reduce_scatter x2, waiting for transfers between devices, back_out(): lax.psum_scatter(back_product(full, weight), 'row', scatter_dimension=0,...  88 us
    all_to_all x2, blocking collectives, back_in(): lax.all_to_all(jnp.stack(jnp.split(partial_value, lax.axis_size('row'), a...  75.6 us
    all_gather x2, waiting for transfers between devices, spread_in(): whole = lax.all_gather(weight, 'row', axis=0, tiled=True)  68 us
    reduce_scatter x2, waiting for transfers between devices, back_in(): lax.psum_scatter(moved, 'col', scatter_dimension=0, tiled=True)  63.5 us
    reduce_scatter x2, waiting for transfers between devices, spread_out(): lax.psum_scatter(jnp.dot(gathered, weight, preferred_element_type=jnp.flo...  61.5 us
    all_gather x2, waiting for transfers between devices, spread_in(): gathered = lax.all_gather(acts, 'col', axis=0, tiled=True)  42.9 us
    all_gather x2, waiting for transfers between devices, spread_out(): gathered = lax.all_gather(branch, 'row', axis=0, tiled=True)  33.9 us
    all_gather x2, waiting for transfers between devices, back_out(): full = lax.all_gather(grad, 'col', axis=0, tiled=True)  27.4 us
  transfers between devices with their start and end apart: 18, of which 15 were waited for; matrix products, arithmetic and copies ran while one was open for 9% of the time, Pallas kernels for 0%

profile of v1, /device:TPU:0, one launch (start us, length us, event | category | flops | bytes accessed | tf_op | source)
XLA Modules:
  0.0 669.1 jit_solution(5201548182185149208)
XLA Ops:
  7.2 1.0 reduce_sum.128
  8.2 11.4 %psum.63 = f32[256]{0:T(256)S(1)} all-reduce(f32[256]{0:T(256)S(1)} %reduce_sum.128), channel_id=1, replica_groups=mesh['row'=4,'col'=8] {'row'}, use_global_device_ids=true, to_apply=%region_1.0 | all-reduce | flops 256 | bytes 2048 | tf_op jit(solution)/shard_map/psum | solution.py:32
  19.6 1.0 multiply_reduce_fusion.6
  20.6 8.0 %psum.64 = f32[256]{0:T(256)S(1)} all-reduce(f32[256]{0:T(256)S(1)} %multiply_reduce_fusion.6), channel_id=1, replica_groups=mesh['row'=4,'col'=8] {'row'}, use_global_device_ids=true, to_apply=%region_3.0 | all-reduce | flops 256 | bytes 2048 | tf_op jit(solution)/shard_map/psum | solution.py:34
  29.5 1.8 add_convert_fusion.1
  31.3 1.9 convert_element_type.69
  33.3 22.7 %all-gather.9.cloned.1.call-done = bf16[2048,272]{0,1:T(8,128)(2,1)} async-done(((bf16[256,272]{0,1:T(8,128)(2,1)}), bf16[2048,272]{0,1:T(8,128)(2,1)}) %all-gather.9.cloned.1.call-update) | async-done | bytes 1114128 | tf_op jit(solution)/shard_map/all_gather | solution.py:66
  56.0 2.3 copy.83
  58.3 3.5 all-to-all-start
  62.1 35.0 %all-gather.11.cloned.1.call-done = bf16[1088,768]{1,0:T(8,128)(2,1)} async-done(((bf16[272,768]{1,0:T(8,128)(2,1)}), bf16[1088,768]{1,0:T(8,128)(2,1)}) %all-gather.11.cloned.1.call-update) | async-done | bytes 1671184 | tf_op jit(solution)/shard_map/all_gather | solution.py:68
  97.1 2.7 convolution_convert_fusion
  103.0 2.0 convolution_convert_fusion.1
  105.0 26.5 %all-gather.13.cloned.1.call-done = bf16[2048,256]{0,1:T(8,128)(2,1)} async-done(((bf16[512,256]{0,1:T(8,128)(2,1)}), bf16[2048,256]{0,1:T(8,128)(2,1)}) %all-gather.13.cloned.1.call-update) | async-done | bytes 1048592 | tf_op jit(solution)/shard_map/all_gather | solution.py:73
  131.5 3.1 fusion.31
  136.3 35.0 %reduce-scatter.11.cloned.1.call-done = f32[256,272]{0,1:T(8,128)} async-done(((f32[2048,272]{0,1:T(8,128)}), f32[256,272]{0,1:T(8,128)}) %reduce-scatter.11.cloned.1.call-update) | async-done | bytes 278544 | tf_op jit(solution)/shard_map/reduce_scatter | solution.py:76
  171.3 1.0 fusion.40
  172.3 9.9 %psum.65 = f32[256]{0:T(256)S(1)} all-reduce(f32[256]{0:T(256)S(1)} %get-tuple-element.68), channel_id=1, replica_groups=mesh['row'=4,'col'=8] {'row'}, use_global_device_ids=true, to_apply=%region_8.9 | all-reduce | flops 256 | bytes 2048 | tf_op jit(solution)/shard_map/psum | solution.py:32
  182.3 8.0 %psum.66 = f32[256]{0:T(256)S(1)} all-reduce(f32[256]{0:T(256)S(1)} %multiply_reduce_fusion.5), channel_id=1, replica_groups=mesh['row'=4,'col'=8] {'row'}, use_global_device_ids=true, to_apply=%region_10.11 | all-reduce | flops 256 | bytes 2048 | tf_op jit(solution)/shard_map/psum | solution.py:34
  192.0 4.4 all-gather.21.cloned.1.call-done
  196.4 4.7 fusion.21
  201.2 20.2 %all-gather.15.cloned.1.call-done = bf16[2048,272]{0,1:T(8,128)(2,1)} async-done(((bf16[256,272]{0,1:T(8,128)(2,1)}), bf16[2048,272]{0,1:T(8,128)(2,1)}) %all-gather.15.cloned.1.call-update) | async-done | bytes 1114128 | tf_op jit(solution)/shard_map/all_gather | solution.py:66
  221.4 2.3 copy.82
  223.7 3.5 all-to-all-start.1
  227.3 33.0 %all-gather.17.cloned.1.call-done = bf16[1088,544]{1,0:T(8,128)(2,1)} async-done(((bf16[272,544]{1,0:T(8,128)(2,1)}), bf16[1088,544]{1,0:T(8,128)(2,1)}) %all-gather.17.cloned.1.call-update) | async-done | bytes 1183760 | tf_op jit(solution)/shard_map/all_gather | solution.py:68
  260.3 57.9 %reduce-scatter.15.cloned.1.call-done = f32[512,544]{0,1:T(8,128)} async-done(((f32[2048,544]{0,1:T(8,128)}), f32[512,544]{0,1:T(8,128)}) %reduce-scatter.15.cloned.1.call-update) | async-done | bytes 1114128 | tf_op jit(solution)/shard_map/reduce_scatter | solution.py:105
  318.2 4.3 fusion.10
  322.5 2.5 fusion.45
  325.4 37.7 %all_to_all.48 = f32[4,512,272]{1,2,0:T(8,128)S(1)} all-to-all(f32[4,512,272]{1,2,0:T(8,128)S(1)} %pad_maximum_fusion), channel_id=1, replica_groups=mesh['row'=4,'col'=8] {'row'}, dimensions={0} | all-to-all | bytes 4456448 | tf_op jit(solution)/shard_map/all_to_all | solution.py:92
  363.1 1.6 copy.78
  364.9 7.5 %all-gather.19.cloned.1.call-done = bf16[2048,544]{0,1:T(8,128)(2,1)} async-done(((bf16[512,544]{0,1:T(8,128)(2,1)}), bf16[2048,544]{0,1:T(8,128)(2,1)}) %all-gather.19.cloned.1.call-update) | async-done | bytes 2228240 | tf_op jit(solution)/shard_map/all_gather | solution.py:73
  372.4 4.0 fusion.23
  376.5 34.6 %reduce-scatter.17.cloned.1.call-done = f32[256,272]{0,1:T(8,128)} async-done(((f32[2048,272]{0,1:T(8,128)}), f32[256,272]{0,1:T(8,128)}) %reduce-scatter.17.cloned.1.call-update) | async-done | bytes 278544 | tf_op jit(solution)/shard_map/reduce_scatter | solution.py:97
  411.1 1.2 multiply_reduce_fusion.1
  412.3 9.8 %all-reduce.2 = (f32[256]{0:T(256)S(1)}, f32[256]{0:T(256)S(1)}) all-reduce(f32[256]{0:T(256)S(1)} %get-tuple-element.53, f32[256]{0:T(256)S(1)} %get-tuple-element.54), channel_id=1, replica_groups=mesh['row'=4,'col'=8] {'row'}, use_global_device_ids=true, to_apply=%region_17.18 | all-reduce | flops 512 | bytes 4096 | tf_op jit(solution)/shard_map/psum | solution.py:46
  422.1 26.6 %reduce-scatter.13.cloned.1.call-done = f32[256,272]{0,1:T(8,128)} async-done(((f32[2048,272]{0,1:T(8,128)}), f32[256,272]{0,1:T(8,128)}) %reduce-scatter.13.cloned.1.call-update) | async-done | bytes 278544 | tf_op jit(solution)/shard_map/reduce_scatter | solution.py:76
  448.6 2.1 fusion.39
  450.8 23.0 %all-gather.23.cloned.1.call-done = bf16[2048,272]{0,1:T(8,128)(2,1)} async-done(((bf16[256,272]{0,1:T(8,128)(2,1)}), bf16[2048,272]{0,1:T(8,128)(2,1)}) %all-gather.23.cloned.1.call-update) | async-done | bytes 1114128 | tf_op jit(solution)/shard_map/all_gather | solution.py:101
  473.8 3.4 fusion.29
  477.3 3.8 fusion.43
  481.1 30.2 %reduce-scatter.19.cloned.1.call-done = f32[512,256]{1,0:T(8,128)} async-done(((f32[2048,256]{1,0:T(8,128)}), f32[512,256]{1,0:T(8,128)}) %reduce-scatter.19.cloned.1.call-update) | async-done | bytes 524304 | tf_op jit(solution)/shard_map/reduce_scatter | solution.py:105
  511.3 1.8 convert_element_type.82
  513.0 1.1 copy.63
  514.2 3.9 multiply_reduce_fusion
  518.1 1.3 multiply_convert_fusion
  520.6 1.3 convolution_bitcast_fusion
  522.0 1.3 copy-done.28
  523.3 1.0 fusion.46
  524.7 37.9 %all_to_all.49 = f32[4,512,272]{1,2,0:T(8,128)S(1)} all-to-all(f32[4,512,272]{1,2,0:T(8,128)S(1)} %pad_maximum_fusion.1), channel_id=1, replica_groups=mesh['row'=4,'col'=8] {'row'}, dimensions={0} | all-to-all | bytes 4456448 | tf_op jit(solution)/shard_map/all_to_all | solution.py:92
  562.7 1.6 copy.79
  564.5 2.8 fusion.41
  567.4 1.2 copy-done.13
  568.6 2.8 fusion.44
  571.4 1.4 fusion.20
  572.8 1.2 pad_maximum_fusion.4
  574.9 2.5 fusion.19
  577.4 1.2 pad_maximum_fusion.3
  581.8 28.9 %reduce-scatter.21.cloned.1.call-done = f32[256,272]{0,1:T(8,128)} async-done(((f32[2048,272]{0,1:T(8,128)}), f32[256,272]{0,1:T(8,128)}) %reduce-scatter.21.cloned.1.call-update) | async-done | bytes 278544 | tf_op jit(solution)/shard_map/reduce_scatter | solution.py:97
  610.7 1.2 multiply_reduce_fusion.2
  611.9 9.9 %all-reduce.1 = (f32[256]{0:T(256)S(1)}, f32[256]{0:T(256)S(1)}) all-reduce(f32[256]{0:T(256)S(1)} %get-tuple-element.51, f32[256]{0:T(256)S(1)} %get-tuple-element.55), channel_id=1, replica_groups=mesh['row'=4,'col'=8] {'row'}, use_global_device_ids=true, to_apply=%region_24.25 | all-reduce | flops 512 | bytes 4096 | tf_op jit(solution)/shard_map/psum | solution.py:46
  621.8 13.9 %psum.71 = f32[4,272]{1,0:T(4,128)S(1)} all-reduce(f32[4,272]{1,0:T(4,128)S(1)} %pad_maximum_fusion.7), channel_id=1, replica_groups=mesh['row'=4,'col'=8] {'col'}, use_global_device_ids=true, to_apply=%region_31.32 | all-reduce | flops 1088 | bytes 8704 | tf_op jit(solution)/shard_map/psum | solution.py:217
  637.0 1.8 multiply_add_fusion
  638.8 19.8 %reduce-scatter.23.cloned.1.call-done = f32[272,768]{1,0:T(8,128)} async-done(((f32[1088,768]{1,0:T(8,128)}), f32[272,768]{1,0:T(8,128)}) %reduce-scatter.23.cloned.1.call-update) | async-done | bytes 835600 | tf_op jit(solution)/shard_map/reduce_scatter | solution.py:87
  658.6 2.7 fusion.18
  661.3 1.3 pad_maximum_fusion.2
  (126 shorter events, 16.3 us)
Async XLA Ops:
  7.2 48.8 %all-gather.9.cloned.1.call-start = ((), (), s32[]{:S(2)}) async-start(), calls=%async_computation.12 | async-start | bytes 1253376 | tf_op jit(solution)/shard_map/all_gather | solution.py:66
  31.3 65.8 %all-gather.11.cloned.1.call-start = ((), (), s32[]{:S(2)}) async-start(), calls=%async_computation.13 | async-start | bytes 2088960 | tf_op jit(solution)/shard_map/all_gather | solution.py:68
  56.0 5.9 copy-start.27
  58.3 38.8 %all-to-all-start = ((bf16[4,512,272]{1,2,0:T(8,128)(2,1)}), bf16[4,512,272]{1,2,0:T(8,128)(2,1)S(1)}, u32[]{:S(2)}, u32[]{:S(2)}) async-start(bf16[4,512,272]{1,2,0:T(8,128)(2,1)} %bitcast.181), calls=%async_computation | async-start | bytes 2228224 | tf_op jit(solution)/shard_map/all_to_all | solution.py:67
  61.9 69.7 %all-gather.13.cloned.1.call-start = ((), (), s32[]{:S(2)}) async-start(), calls=%async_computation.14 | async-start | bytes 1310720 | tf_op jit(solution)/shard_map/all_gather | solution.py:73
  62.1 39.8 %copy-start.8 = (pred[512,512]{0,1:T(8,128)(4,1)}, pred[512,512]{0,1:T(8,128)(4,1)S(1)}, u32[]{:S(2)}) copy-start(pred[512,512]{0,1:T(8,128)(4,1)S(1)} %fusion.11) | copy-start | bytes 786436
  100.1 1.9 copy-start.11
  101.0 2.0 copy-start
  103.0 28.5 %copy-start.5 = (f32[256,272]{0,1:T(8,128)S(1)}, f32[256,272]{0,1:T(8,128)}, u32[]{:S(2)}) copy-start(f32[256,272]{0,1:T(8,128)} %param.16) | copy-start | bytes 835588
  105.0 66.3 %reduce-scatter.11.cloned.1.call-start = ((), (), s32[]{:S(2)}) async-start(), calls=%async_computation.15 | async-start | bytes 2506752 | tf_op jit(solution)/shard_map/reduce_scatter | solution.py:76
  134.6 1.0 copy-start.19
  134.6 36.7 %copy-start.2 = (f32[256,272]{0,1:T(8,128)S(1)}, f32[256,272]{0,1:T(8,128)}, u32[]{:S(2)}) copy-start(f32[256,272]{0,1:T(8,128)} %param.13) | copy-start | bytes 835588
  134.6 56.5 %copy-start.14 = (f32[272,544]{1,0:T(8,128)S(1)}, f32[272,544]{1,0:T(8,128)}, u32[]{:S(2)}) copy-start(f32[272,544]{1,0:T(8,128)} %param.17) | copy-start | bytes 1775620
  134.7 61.7 %copy-start.3 = (f32[544,272]{0,1:T(8,128)S(1)}, f32[544,272]{0,1:T(8,128)}, u32[]{:S(2)}) copy-start(f32[544,272]{0,1:T(8,128)} %param.18) | copy-start | bytes 1775620
  134.7 61.7 %all-gather.21.cloned.1.call-start = ((), (), s32[]{:S(2)}) async-start(), calls=%async_computation.20 | async-start | bytes 1253376 | tf_op jit(solution)/shard_map/all_gather | solution.py:101
  136.3 85.1 %all-gather.15.cloned.1.call-start = ((), (), s32[]{:S(2)}) async-start(), calls=%async_computation.16 | async-start | bytes 1253376 | tf_op jit(solution)/shard_map/all_gather | solution.py:66
  191.1 69.2 %all-gather.17.cloned.1.call-start = ((), (), s32[]{:S(2)}) async-start(), calls=%async_computation.17 | async-start | bytes 1740800 | tf_op jit(solution)/shard_map/all_gather | solution.py:68
  191.9 126.2 %reduce-scatter.15.cloned.1.call-start = ((), (), s32[]{:S(2)}) async-start(), calls=%async_computation.21 | async-start | bytes 5570560 | tf_op jit(solution)/shard_map/reduce_scatter | solution.py:105
  223.7 94.4 %all-to-all-start.1 = ((bf16[4,512,272]{1,2,0:T(8,128)(2,1)}), bf16[4,512,272]{1,2,0:T(8,128)(2,1)S(1)}, u32[]{:S(2)}, u32[]{:S(2)}) async-start(bf16[4,512,272]{1,2,0:T(8,128)(2,1)} %bitcast.190), calls=%async_computation.2 | async-start | bytes 2228224 | tf_op jit(solution)/shard_map/all_to_all | solution.py:67
  227.3 145.1 %all-gather.19.cloned.1.call-start = ((), (), s32[]{:S(2)}) async-start(), calls=%async_computation.18 | async-start | bytes 2785280 | tf_op jit(solution)/shard_map/all_gather | solution.py:73
  322.5 88.6 %reduce-scatter.17.cloned.1.call-start = ((), (), s32[]{:S(2)}) async-start(), calls=%async_computation.22 | async-start | bytes 2506752 | tf_op jit(solution)/shard_map/reduce_scatter | solution.py:97
  364.7 83.9 %reduce-scatter.13.cloned.1.call-start = ((), (), s32[]{:S(2)}) async-start(), calls=%async_computation.19 | async-start | bytes 2506752 | tf_op jit(solution)/shard_map/reduce_scatter | solution.py:76
  376.4 97.4 %all-gather.23.cloned.1.call-start = ((), (), s32[]{:S(2)}) async-start(), calls=%async_computation.23 | async-start | bytes 1253376 | tf_op jit(solution)/shard_map/all_gather | solution.py:101
  450.8 60.5 %reduce-scatter.19.cloned.1.call-start = ((), (), s32[]{:S(2)}) async-start(), calls=%async_computation.24 | async-start | bytes 2621440 | tf_op jit(solution)/shard_map/reduce_scatter | solution.py:105
  477.2 96.8 %reduce-scatter.25.cloned.1.call-start = ((), (), s32[]{:S(2)}) async-start(), calls=%async_computation.27 | async-start | bytes 3481600
  481.0 33.1 %copy-start.9 = (pred[512,512]{0,1:T(8,128)(4,1)S(1)}, pred[512,512]{0,1:T(8,128)(4,1)}, u32[]{:S(2)}) copy-start(pred[512,512]{0,1:T(8,128)(4,1)} %copy-done.8) | copy-start | bytes 786436
  481.0 33.1 %copy-start.12 = (bf16[512,768]{0,1:T(8,128)(2,1)S(1)}, bf16[512,768]{0,1:T(8,128)(2,1)}, u32[]{:S(2)}) copy-start(bf16[512,768]{0,1:T(8,128)(2,1)} %copy-done.11) | copy-start | bytes 2359300
  481.0 129.7 %reduce-scatter.21.cloned.1.call-start = ((), (), s32[]{:S(2)}) async-start(), calls=%async_computation.25 | async-start | bytes 2506752 | tf_op jit(solution)/shard_map/reduce_scatter | solution.py:97
  514.2 3.9 copy-start.1
  521.8 1.4 copy-start.28
  564.3 94.4 %reduce-scatter.23.cloned.1.call-start = ((), (), s32[]{:S(2)}) async-start(), calls=%async_computation.26 | async-start | bytes 4177920 | tf_op jit(solution)/shard_map/reduce_scatter | solution.py:87
  567.3 1.2 copy-start.13
  568.6 2.8 copy-start.17
  571.4 1.4 copy-start.22
  572.8 1.3 copy-start.15
  572.8 2.1 copy-start.18
  577.4 1.8 copy-start.4
  577.4 2.1 copy-start.7
  577.4 2.6 copy-start.6
  577.4 2.6 copy-start.23
  580.0 58.8 %copy-start.21 = (f32[256,272]{0,1:T(8,128)}, f32[256,272]{0,1:T(8,128)S(1)}, u32[]{:S(2)}) copy-start(f32[256,272]{0,1:T(8,128)S(1)} %fusion.42) | copy-start | bytes 835588
  580.0 55.7 %copy-start.24 = (f32[4,272]{1,0:T(4,128)S(1)}, f32[4,272]{1,0:T(4,128)}, u32[]{:S(2)}) copy-start(f32[4,272]{1,0:T(4,128)} %param.19) | copy-start | bytes 13060
  580.0 55.7 %copy-start.26 = (f32[2,4,272]{2,1,0:T(4,128)S(1)}, f32[2,4,272]{2,1,0:T(4,128)}, u32[]{:S(2)}) copy-start(f32[2,4,272]{2,1,0:T(4,128)} %param.24) | copy-start | bytes 26116
  580.0 57.0 %copy-start.20 = (f32[256,272]{0,1:T(8,128)S(1)}, f32[256,272]{0,1:T(8,128)}, u32[]{:S(2)}) copy-start(f32[256,272]{0,1:T(8,128)} %get-tuple-element.67) | copy-start | bytes 835588
  580.0 78.6 %copy-start.10 = (f32[272,768]{1,0:T(8,128)S(1)}, f32[272,768]{1,0:T(8,128)}, u32[]{:S(2)}) copy-start(f32[272,768]{1,0:T(8,128)} %param.15) | copy-start | bytes 2506756
  580.0 78.6 %copy-start.16 = (f32[2,272,768]{2,1,0:T(8,128)S(1)}, f32[2,272,768]{2,1,0:T(8,128)}, u32[]{:S(2)}) copy-start(f32[2,272,768]{2,1,0:T(8,128)} %param.20) | copy-start | bytes 5013508
  635.8 25.6 %copy-start.25 = (f32[4,272]{1,0:T(4,128)}, f32[4,272]{1,0:T(4,128)S(1)}, u32[]{:S(2)}) copy-start(f32[4,272]{1,0:T(4,128)S(1)} %psum.71) | copy-start | bytes 13060
Sparse Core Ops, SparseCore 0:
  31.4 24.5 all-gather.8
  58.4 38.7 all-gather.10
  105.1 26.3 all-gather.12
  134.8 36.4 reduce-scatter.10
  173.3 23.0 all-gather.20
  198.4 22.9 all-gather.14
  223.8 36.4 all-gather.16
  263.4 54.7 reduce-scatter.14
  322.6 49.7 all-gather.18
  374.5 36.4 reduce-scatter.16
  413.4 35.2 reduce-scatter.12
  450.9 22.8 all-gather.22
  477.3 33.8 reduce-scatter.18
  514.7 57.2 reduce-scatter.24
  574.2 36.4 reduce-scatter.20
  614.2 44.4 reduce-scatter.22
